TPU v7x, 32 devices: a whole 2x2x4 slice. The times are simulated.
32 devices in a mesh: seq: 8 (over y, x, core), head: 4 (over z).
Axes of the slice: x: 2, y: 2, z: 4, core: 2. Of those that a mesh axis runs over, the one named last changes fastest.
Arguments:
- frames: bfloat16 [8192, 1024], P(('seq', 'head')), may hold values from -6 to 6
- cotangent: bfloat16 [8192, 1024], P(('seq', 'head')), may hold values from -6 to 6
- norm_gain: float32 [1024], replicated, may hold values from 0.25 to 1.75
- w_qkv: bfloat16 [3, 1024, 1024], replicated
- w_out: bfloat16 [1024, 1024], replicated, may hold values from -0.1875 to 0.1875
Outputs:
- output: bfloat16 [8192, 1024], P(('seq', 'head'))
- grad_frames: bfloat16 [8192, 1024], P(('seq', 'head'))
- grad_qkv: float32 [3, 1024, 1024], P(None, 'seq', 'head')
- grad_out: float32 [1024, 1024], P('seq', 'head')
All inputs are finite; a program needn't handle non-finite values.
Results may differ from a plain program's by a relative error of at most 0.015.
Values may be sent and summed in bfloat16 or wider, within the bound.
A program may use at most 128 MiB of HBM per device.

v0:
```python
import jax
import jax.numpy as jnp
from jax import lax
from jax.sharding import PartitionSpec as P

HEAD_SIZE = 128
WINDOW = 128
EPSILON = 1e-05
MASKED = -1e30


def with_halo(shard, sides, width):
    for axis, dim in sides:
        devices, length = (lax.axis_size(axis), shard.shape[dim])
        up = [(i, (i + 1) % devices) for i in range(devices - 1)]
        down = [(j, i) for i, j in up]
        last = lax.slice_in_dim(shard, length - width, length, axis=dim)
        first = lax.slice_in_dim(shard, 0, width, axis=dim)
        before = lax.ppermute(last, axis, up)
        after = lax.ppermute(first, axis, down)
        shard = jnp.concatenate([before, shard, after], axis=dim)
    return shard


def layer_norm(values, norm_gain):
    average = jnp.mean(values, axis=-1, keepdims=True)
    centered = values - average
    variance = jnp.mean(centered * centered, axis=-1, keepdims=True)
    return centered * lax.rsqrt(variance + EPSILON) * norm_gain


def norm_grad(frames, norm_gain, upstream):
    _, pullback = jax.vjp(lambda v: layer_norm(v, norm_gain), frames.astype(jnp.float32))
    return pullback(upstream.astype(jnp.float32))[0]


def attention(query_rows, key_rows, value_rows, offset, frame_total):
    length, channels = query_rows.shape
    head_count = channels // HEAD_SIZE
    block_rows = min(length, 512)
    block_count = length // block_rows
    key_span = block_rows + 2 * WINDOW
    score_scale = HEAD_SIZE ** (-0.5)

    def one_block(block_index):
        anchor = block_index * block_rows
        query_part = lax.dynamic_slice_in_dim(query_rows, anchor, block_rows, 0).reshape(
            block_rows, head_count, HEAD_SIZE
        )
        key_part = lax.dynamic_slice_in_dim(key_rows, anchor, key_span, 0).reshape(
            key_span, head_count, HEAD_SIZE
        )
        value_part = lax.dynamic_slice_in_dim(value_rows, anchor, key_span, 0).reshape(
            key_span, head_count, HEAD_SIZE
        )
        query_pos = offset + anchor + jnp.arange(block_rows, dtype=jnp.int32)
        key_pos = offset + anchor - WINDOW + jnp.arange(key_span, dtype=jnp.int32)
        distance = query_pos[:, None] - key_pos[None, :]
        allowed = (
            (jnp.abs(distance) <= WINDOW)
            & (key_pos >= 0)[None, :]
            & (key_pos < frame_total)[None, :]
        )
        scores = (
            jnp.einsum("qhe,khe->hqk", query_part, key_part, precision=lax.Precision.HIGHEST)
            * score_scale
        )
        scores = jnp.where(allowed[None], scores, MASKED)
        row_max = lax.stop_gradient(jnp.max(scores, axis=-1, keepdims=True))
        weights = jnp.exp(scores - row_max)
        weights = weights / jnp.sum(weights, axis=-1, keepdims=True)
        combined = jnp.einsum("hqk,khe->qhe", weights, value_part, precision=lax.Precision.HIGHEST)
        return combined.reshape(block_rows, channels)

    results = lax.map(jax.checkpoint(one_block), jnp.arange(block_count, dtype=jnp.int32))
    return results.reshape(length, channels)


def attention_grad(query_rows, key_rows, value_rows, offset, frame_total, upstream):
    _, pullback = jax.vjp(
        lambda a, b, c: attention(a, b, c, offset, frame_total), query_rows, key_rows, value_rows
    )
    return pullback(upstream.astype(jnp.float32))


def to_heads(stacked):
    return lax.all_to_all(stacked, "head", split_axis=2, concat_axis=1, tiled=True)


def to_time(stacked):
    return lax.all_to_all(stacked, "head", split_axis=1, concat_axis=2, tiled=True)


def sum_columns(term):
    return lax.psum_scatter(
        term.astype(jnp.bfloat16), "head", scatter_dimension=2, tiled=True
    ).astype(jnp.float32)


def sum_rows(term):
    return lax.psum_scatter(
        term.astype(jnp.bfloat16), "seq", scatter_dimension=1, tiled=True
    ).astype(jnp.float32)


def shards(frames, cotangent, norm_gain, w_qkv, w_out):
    frame_rows = frames.shape[0]
    head_groups = lax.axis_size("head")
    frame_total = lax.axis_size("seq") * head_groups * frame_rows
    grad_scale = frame_total ** (-0.5)
    normed = layer_norm(frames.astype(jnp.float32), norm_gain).astype(jnp.bfloat16)
    projected = jnp.einsum("td,cdf->ctf", normed, w_qkv, preferred_element_type=jnp.float32).astype(
        jnp.bfloat16
    )
    offset = lax.axis_index("seq") * (head_groups * frame_rows)
    local_qkv = to_heads(projected)
    bordered = with_halo(local_qkv[1:], (("seq", 1),), WINDOW)
    query_rows = local_qkv[0].astype(jnp.float32)
    key_rows = bordered[0].astype(jnp.float32)
    value_rows = bordered[1].astype(jnp.float32)
    length = query_rows.shape[0]
    attended = attention(query_rows, key_rows, value_rows, offset, frame_total).astype(jnp.bfloat16)
    mixed_rows = to_time(attended[None])[0]
    output = (
        frames.astype(jnp.float32) + jnp.dot(mixed_rows, w_out, preferred_element_type=jnp.float32)
    ).astype(jnp.bfloat16)
    grad_mixed = jnp.einsum(
        "tf,df->td", cotangent, w_out, preferred_element_type=jnp.float32
    ).astype(jnp.bfloat16)
    grad_attended = to_heads(grad_mixed[None])[0]
    grad_query, grad_keys, grad_values = attention_grad(
        query_rows, key_rows, value_rows, offset, frame_total, grad_attended
    )
    pair_grads = jnp.stack([grad_keys, grad_values])
    edge_grads = jnp.concatenate([pair_grads[:, :WINDOW], pair_grads[:, length + WINDOW :]], axis=1)
    returned = with_halo(edge_grads.astype(jnp.bfloat16), (("seq", 1),), WINDOW).astype(
        edge_grads.dtype
    )
    interior = pair_grads[:, WINDOW : length + WINDOW]
    interior = interior.at[:, :WINDOW].add(returned[:, :WINDOW])
    interior = interior.at[:, length - WINDOW :].add(returned[:, 3 * WINDOW :])
    grad_local = jnp.concatenate([grad_query[None], interior], axis=0).astype(jnp.bfloat16)
    grad_time = to_time(grad_local)
    grad_normed = jnp.einsum(
        "ctf,cdf->td", grad_time, w_qkv, preferred_element_type=jnp.float32
    ).astype(jnp.bfloat16)
    grad_frames = (
        cotangent.astype(jnp.float32) + norm_grad(frames, norm_gain, grad_normed)
    ).astype(jnp.bfloat16)
    out_term = (
        jnp.einsum("td,tf->df", mixed_rows, cotangent, preferred_element_type=jnp.float32)[None]
        * grad_scale
    )
    grad_out = sum_rows(sum_columns(out_term))[0]
    time_term = (
        jnp.einsum("td,ctf->cdf", normed, grad_time, preferred_element_type=jnp.float32)
        * grad_scale
    )
    grad_qkv = sum_rows(sum_columns(time_term))
    return (output, grad_frames, grad_qkv, grad_out)


def solution(mesh):
    in_specs = (P(("seq", "head"), None), P(("seq", "head"), None), P(), P(), P())
    out_specs = (
        P(("seq", "head"), None),
        P(("seq", "head"), None),
        P(None, "seq", "head"),
        P("seq", "head"),
    )
    return jax.shard_map(shards, mesh=mesh, in_specs=in_specs, out_specs=out_specs, check_vma=False)
```

profile of v0, /device:TPU:0, one launch (start us, length us, event | category | flops | bytes accessed | tf_op | source)
XLA Modules:
  0.0 544.6 jit_solution(4253332027485808211)
XLA Ops:
  10.6 2.0 copy.117
  13.1 4.8 reduce.5
  18.9 6.3 %all-to-all-start.2 = ((bf16[4,2,32768]{2,1,0:T(2,128)(2,1)}), bf16[4,2,32768]{2,1,0:T(2,128)(2,1)S(1)}, u32[]{:S(2)}, u32[]{:S(2)}) async-start(bf16[4,2,32768]{2,1,0:T(2,128)(2,1)} %reshape.388), calls=%async_computation.2 | async-start | bytes 1048576 | tf_op jit(solution)/shard_map/all_to_all | solution.py:87
  26.8 5.9 %fusion.34 = bf16[3,256,1024]{2,1,0:T(8,128)(2,1)} fusion(bf16[3,1024,1024]{2,1,0:T(8,128)(2,1)} %param.16, bf16[256,1024]{1,0:T(8,128)(2,1)S(1)} %copy-done.13, f32[1024]{0:T(1024)S(1)} %copy-done.28, f32[256]{0:T(256)S(1)} %fusion.53, f32[256]{0:T(256)S(1)} %broadcast_multiply_fusion), kind=kOutput, calls=%fused_computation.76 | convolution fusion | flops 1612709888 | bytes 8394752 | tf_op jit(solution)/shard_map/td,cdf->ctf/dot_general | solution.py:112
  32.6 4.1 copy.107
  36.8 2.9 all-to-all-done.2
  39.7 4.5 all-to-all-start
  44.2 2.2 reshape.389
  47.9 44.0 %all-to-all-done = bf16[3,256,1024]{1,0,2:T(4,128)(2,1)} async-done(((bf16[3,256,1024]{1,0,2:T(4,128)(2,1)}), bf16[3,256,1024]{1,0,2:T(4,128)(2,1)}, u32[]{:S(2)}, u32[]{:S(2)}) %all-to-all-start) | async-done | bytes 1572896 | tf_op jit(solution)/shard_map/all_to_all | solution.py:87
  92.0 4.1 copy.109
  96.1 2.3 slice.104
  105.3 2.1 bitcast_convert_fusion
  107.4 2.5 copy.113
  111.7 29.2 %while.32 = (s32[]{:T(128)}, bf16[2,512,256]{2,1,0:T(8,128)(2,1)}, s32[2]{0:T(128)S(1)}, f32[1280,256]{0,1:T(8,128)}, s32[]{:T(128)}, /*index=5*/f32[1024,256]{0...) while((s32[]{:T(128)}, bf16[2,512,256]{2,1,0:T(8,128)(2,1)}, ...), condition=%wide.region_5.6_spmd, body=%wide.region_2.5_spmd.sunk | while | flops 2426537472 | bytes 25986388 | solution.py:75
  113.6 2.4 constant_dynamic-slice_fusion.15
  117.1 3.3 fusion.114
  121.3 4.1 fusion.116
  128.2 2.4 constant_dynamic-slice_fusion.15
  131.7 3.3 fusion.114
  135.9 4.1 fusion.116
  142.8 4.7 reduce.4
  149.4 4.1 all-to-all-start.1
  157.0 70.9 %while.33 = (s32[]{:T(128)}, f32[1024,256]{1,0:T(8,128)}, f32[1280,256]{0,1:T(8,128)}, f32[1280,256]{0,1:T(8,128)}, s32[2]{0:T(128)S(1)}, /*index=5*/f32[2,512,2...) while((s32[]{:T(128)}, f32[1024,256]{1,0:T(8,128)}, ...), condition=%wide.region_10.11_spmd, body=%wide.region_6.10_spmd.sunk | while | flops 6061953024 | bytes 89728512 | solution.py:75
  175.2 3.3 fusion.130
  179.6 3.9 multiply_reduce_fusion.2
  186.7 2.8 fusion.133
  189.9 3.4 fusion.132
  204.6 3.3 fusion.130
  208.9 3.9 multiply_reduce_fusion.2
  216.1 2.8 fusion.133
  219.2 3.4 fusion.132
  227.9 3.9 copy.138
  231.8 2.1 copy.139
  233.9 2.2 reshape.391
  238.3 3.3 fusion.29
  241.7 4.1 fusion.27
  245.9 4.8 collective-permute-start.2
  256.7 2.2 pad_maximum_fusion.1
  258.9 74.3 %all_to_all.57 = bf16[3,1024,256]{2,0,1:T(4,128)(2,1)S(1)} all-to-all(bf16[3,1024,256]{2,0,1:T(4,128)(2,1)S(1)} %pad_maximum_fusion.1), channel_id=1, replica_groups=mesh['seq'=8,'head'=4] {'head'}, dimensions={1} | all-to-all | bytes 3145728 | tf_op jit(solution)/shard_map/all_to_all | solution.py:91
  333.2 2.7 copy.156
  335.9 3.8 all_to_all.52
  339.7 6.1 %fusion.26 = bf16[3,1024,1024]{1,2,0:T(8,128)(2,1)} fusion(bf16[3,256,1024]{2,1,0:T(8,128)(2,1)} %all_to_all.52, bf16[256,1024]{1,0:T(8,128)(2,1)S(1)} %copy-done.14, f32[1024]{0:T(1024)S(1)} %copy-done.29, f32[256]{0:T(256)S(1)} %copy-done.25, f32[256]{0:T(256)S(1)} %copy-done.23), kind=kOutput, calls=%fused_computation.55 | convolution fusion | flops 1618214912 | bytes 8394752 | tf_op jit(solution)/shard_map/td,ctf->cdf/dot_general | solution.py:156
  346.6 109.6 %reduce-scatter.7.cloned.1.call-done = bf16[3,1024,256]{1,2,0:T(8,128)(2,1)} async-done(((bf16[3,1024,1024]{1,2,0:T(8,128)(2,1)}), bf16[3,1024,256]{1,2,0:T(8,128)(2,1)}) %reduce-scatter.7.cloned.1.call-update) | async-done | bytes 1572880 | tf_op jit(solution)/shard_map/reduce_scatter | solution.py:95
  456.2 4.4 copy.140
  460.6 3.2 copy.153
  465.3 5.1 fusion.43
  472.0 21.9 %reduce-scatter.11.cloned.1.call-done = bf16[1,128,256]{2,1,0:T(8,128)(2,1)} async-done(((bf16[1,1024,256]{2,1,0:T(8,128)(2,1)}), bf16[1,128,256]{2,1,0:T(8,128)(2,1)}) %reduce-scatter.11.cloned.1.call-update) | async-done | bytes 65552 | tf_op jit(solution)/shard_map/reduce_scatter | solution.py:101
  495.5 40.1 %reduce-scatter.13.cloned.1.call-done = bf16[128,768]{1,0:T(8,128)(2,1)} async-done(((bf16[1024,768]{1,0:T(8,128)(2,1)}), bf16[128,768]{1,0:T(8,128)(2,1)}) %reduce-scatter.13.cloned.1.call-update) | async-done | bytes 196624
  (200 shorter events, 78.3 us)
Async XLA Ops:
  7.2 1.6 copy-start
  10.5 14.7 %copy-start.13 = (bf16[256,1024]{1,0:T(8,128)(2,1)S(1)}, bf16[256,1024]{1,0:T(8,128)(2,1)}, u32[]{:S(2)}) copy-start(bf16[256,1024]{1,0:T(8,128)(2,1)} %param.13) | copy-start | bytes 1572868
  10.6 16.2 %copy-start.28 = (f32[1024]{0:T(1024)S(1)}, f32[1024]{0:T(1024)}, u32[]{:S(2)}) copy-start(f32[1024]{0:T(1024)} %param.15) | copy-start | bytes 12292
  18.9 20.8 %all-to-all-start.2 = ((bf16[4,2,32768]{2,1,0:T(2,128)(2,1)}), bf16[4,2,32768]{2,1,0:T(2,128)(2,1)S(1)}, u32[]{:S(2)}, u32[]{:S(2)}) async-start(bf16[4,2,32768]{2,1,0:T(2,128)(2,1)} %reshape.388), calls=%async_computation.2 | async-start | bytes 1048576 | tf_op jit(solution)/shard_map/all_to_all | solution.py:87
  25.4 0.9 copy-start.22
  39.7 4.5 copy-start.17
  39.7 52.3 %all-to-all-start = ((bf16[3,256,1024]{1,0,2:T(4,128)(2,1)}), bf16[3,256,1024]{1,0,2:T(4,128)(2,1)}, u32[]{:S(2)}, u32[]{:S(2)}) async-start(bf16[3,256,1024]{1,0,2:T(4,128)(2,1)} %copy.107), calls=%async_computation | async-start | bytes 4194304 | tf_op jit(solution)/shard_map/all_to_all | solution.py:87
  102.4 7.5 %collective-permute-start = (bf16[2,128,256]{1,2,0:T(8,128)(2,1)}, bf16[2,128,256]{1,2,0:T(8,128)(2,1)S(1)}, u32[]{:S(2)}, u32[]{:S(2)}) collective-permute-start(bf16[2,128,256]{1,2,0:T(8,128)(2,1)} %get-tuple-element.473), channel_id=1, source_target_pairs={{0,4},{4,8},{8,12},{12,16},{16,20},{20,24},{24,28},{1,5},{5,9},{9,... | collective-permute-start | bytes 393224 | tf_op jit(solution)/shard_map/ppermute | solution.py:19
  103.7 6.2 %collective-permute-start.1 = (bf16[2,128,256]{1,2,0:T(8,128)(2,1)S(1)}, bf16[2,128,256]{1,2,0:T(8,128)(2,1)S(1)}, u32[]{:S(2)}, u32[]{:S(2)}) collective-permute-start(bf16[2,128,256]{1,2,0:T(8,128)(2,1)S(1)} %get-tuple-element.474), channel_id=1, source_target_pairs={{4,0},{8,4},{12,8},{16,12},{20,16},{24,20},{28,24},{5,1},{9,5},{13... | collective-permute-start | bytes 393224 | tf_op jit(solution)/shard_map/ppermute | solution.py:20
  117.0 4.2 copy-start.12
  121.3 4.2 copy-start.20
  125.5 0.8 copy-start.21
  131.7 4.2 copy-start.12
  135.9 4.2 copy-start.20
  149.4 84.5 %all-to-all-start.1 = ((bf16[4,2,32768]{2,1,0:T(2,128)(2,1)}), bf16[4,2,32768]{2,1,0:T(2,128)(2,1)}, u32[]{:S(2)}, u32[]{:S(2)}) async-start(bf16[4,2,32768]{2,1,0:T(2,128)(2,1)} %reshape.390), calls=%async_computation.1 | async-start | bytes 1048576 | tf_op jit(solution)/shard_map/all_to_all | solution.py:91
  153.6 192.3 %reduce-scatter.9.cloned.1.call-start = ((), (), s32[]{:S(2)}) async-start(), calls=%async_computation.9 | async-start | bytes 2621440 | tf_op jit(solution)/shard_map/reduce_scatter | solution.py:95
  175.2 4.2 copy-start.1
  178.5 1.0 copy-start.2
  186.7 2.8 copy-start.3
  186.7 2.8 copy-start.5
  189.8 3.4 copy-start.4
  189.9 3.4 copy-start.6
  189.9 3.4 copy-start.8
  204.6 4.2 copy-start.1
  207.9 1.0 copy-start.2
  216.1 2.8 copy-start.3
  216.1 2.8 copy-start.5
  219.2 3.4 copy-start.4
  219.2 3.4 copy-start.6
  219.2 3.4 copy-start.8
  227.9 3.9 copy-start.7
  238.3 3.3 copy-start.15
  241.6 10.4 %copy-start.9 = (f32[1024,256]{1,0:T(8,128)S(1)}, f32[1024,256]{1,0:T(8,128)}, u32[]{:S(2)}) copy-start(f32[1024,256]{1,0:T(8,128)} %get-tuple-element.325) | copy-start | bytes 3145732
  241.6 214.6 %reduce-scatter.7.cloned.1.call-start = ((), (), s32[]{:S(2)}) async-start(), calls=%async_computation.8 | async-start | bytes 7864320 | tf_op jit(solution)/shard_map/reduce_scatter | solution.py:95
  241.7 11.2 %copy-start.10 = (f32[1,1280,256]{2,0,1:T(1,128)S(1)}, f32[1,1280,256]{2,0,1:T(1,128)}, u32[]{:S(2)}) copy-start(f32[1,1280,256]{2,0,1:T(1,128)} %copy.138) | copy-start | bytes 3932164
  241.7 11.2 %copy-start.11 = (f32[1,1280,256]{2,0,1:T(1,128)S(1)}, f32[1,1280,256]{2,0,1:T(1,128)}, u32[]{:S(2)}) copy-start(f32[1,1280,256]{2,0,1:T(1,128)} %copy.139) | copy-start | bytes 3932164
  245.9 8.9 %collective-permute-start.2 = (bf16[2,128,256]{2,0,1:T(2,128)(2,1)S(1)}, bf16[2,128,256]{2,0,1:T(2,128)(2,1)S(1)}, u32[]{:S(2)}, u32[]{:S(2)}) collective-permute-start(bf16[2,128,256]{2,0,1:T(2,128)(2,1)S(1)} %get-tuple-element.469), channel_id=1, source_target_pairs={{0,4},{4,8},{8,12},{12,16},{16,20},{20,24},{24,28},{1,5},{5,9},{9,... | collective-permute-start | bytes 393224 | tf_op jit(solution)/shard_map/ppermute | solution.py:19
  250.7 4.5 collective-permute-start.3
  333.2 6.5 %copy-start.14 = (bf16[256,1024]{1,0:T(8,128)(2,1)S(1)}, bf16[256,1024]{1,0:T(8,128)(2,1)}, u32[]{:S(2)}) copy-start(bf16[256,1024]{1,0:T(8,128)(2,1)} %param.13) | copy-start | bytes 1572868
  333.2 6.5 %copy-start.23 = (f32[256]{0:T(256)S(1)}, f32[256]{0:T(256)}, u32[]{:S(2)}) copy-start(f32[256]{0:T(256)} %copy-done.22) | copy-start | bytes 3076
  333.2 6.5 %copy-start.25 = (f32[256]{0:T(256)S(1)}, f32[256]{0:T(256)}, u32[]{:S(2)}) copy-start(f32[256]{0:T(256)} %copy-done.24) | copy-start | bytes 3076
  333.2 6.5 %copy-start.29 = (f32[1024]{0:T(1024)S(1)}, f32[1024]{0:T(1024)}, u32[]{:S(2)}) copy-start(f32[1024]{0:T(1024)} %param.15) | copy-start | bytes 12292
  345.8 148.2 %reduce-scatter.11.cloned.1.call-start = ((), (), s32[]{:S(2)}) async-start(), calls=%async_computation.10 | async-start | bytes 589824 | tf_op jit(solution)/shard_map/reduce_scatter | solution.py:101
  346.5 189.0 %reduce-scatter.13.cloned.1.call-start = ((), (), s32[]{:S(2)}) async-start(), calls=%async_computation.11 | async-start | bytes 1769472
  460.6 3.2 copy-start.16
  463.8 1.5 copy-start.19
  465.3 5.1 copy-start.27
  465.3 5.5 %copy-start.18 = (bf16[256,1024]{1,0:T(8,128)(2,1)S(1)}, bf16[256,1024]{1,0:T(8,128)(2,1)}, u32[]{:S(2)}) copy-start(bf16[256,1024]{1,0:T(8,128)(2,1)} %param.14) | copy-start | bytes 1572868
  (3 other events, 1.9 us)
Sparse Core Ops, SparseCore 0:
  241.7 66.6 reduce-scatter.8
  345.9 110.2 reduce-scatter.6
  459.3 34.6 reduce-scatter.10
  497.1 38.3 reduce-scatter.12
where the time goes:
time: 553 us; the launch traced here: 545 us
  waiting for transfers between devices  220 us (40%)
  local copies, waits for them, and re-layouts  90.1 us (16%)
  blocking collectives  74.3 us (13%)
  matrix products  68.8 us (12%)
  other arithmetic  37.8 us (7%)
  starting transfers between devices  24 us (4%)
  loops' own time  15.4 us (3%)
  between operations  14.6 us (3%)
    reduce_scatter x2, waiting for transfers between devices, sum_columns(): lax.psum_scatter(term.astype(jnp.bfloat16), 'head', scatter_dimension=2,...  110 us
    all_to_all x1, blocking collectives, to_time(): lax.all_to_all(stacked, 'head', split_axis=1, concat_axis=2, tiled=True)  74.3 us
    all_to_all x2, waiting for transfers between devices, to_heads(): lax.all_to_all(stacked, 'head', split_axis=2, concat_axis=1, tiled=True)  47 us
    unnamed x5, waiting for transfers between devices  40.8 us
    dot_general x8, matrix products, one_block(): jnp.einsum('qhe,khe->hqk', query_part, key_part, precision=lax.Precision....  23.7 us
    reduce_scatter x1, waiting for transfers between devices, sum_rows(): lax.psum_scatter(term.astype(jnp.bfloat16), 'seq', scatter_dimension=1, t...  21.9 us
    dot_general x6, matrix products, one_block(): jnp.einsum('hqk,khe->qhe', weights, value_part, precision=lax.Precision.H...  21.4 us
    unnamed x51, local copies, waits for them, and re-layouts  21.2 us
  transfers between devices with their start and end apart: 11, of which 6 were waited for; matrix products, arithmetic and copies ran while one was open for 22% of the time, Pallas kernels for 0%

commit v1 on v0

--- a/solution.py
+++ b/solution.py
@@ -84,7 +84,10 @@
 
 
 def to_heads(stacked):
-    return lax.all_to_all(stacked, "head", split_axis=2, concat_axis=1, tiled=True)
+    return jnp.concatenate(
+        lax.all_to_all(jnp.stack(jnp.split(stacked, lax.axis_size("head"), axis=2)), "head", 0, 0),
+        axis=1,
+    )
 
 
 def to_time(stacked):

time: 553 us -> 518 us (0.937)
  local copies, waits for them, and re-layouts: 90.1 us -> 77.1 us
  loops' own time: 15.4 us -> 4.11 us
    another operation x2, loops' own time: 15.4 us -> 4.11 us  [attention(): lax.map(jax.checkpoint(one_block), jnp.arange(block_count, dtype=jnp.int32))]
    unnamed x51 -> x47, local copies, waits for them, and re-layouts: 21.2 us -> 17.4 us
  transfers between devices with their start and end apart: 11 -> 11, of which waited for: 6 -> 5; matrix products, arithmetic and copies ran while one was open for 22% -> 22% of each run, Pallas kernels for 0% -> 0%
where the time goes in v1:
time: 518 us; the launch traced here: 511 us
  waiting for transfers between devices  215 us (42%)
  local copies, waits for them, and re-layouts  77.1 us (15%)
  blocking collectives  73.8 us (14%)
  matrix products  67.6 us (13%)
  other arithmetic  34.6 us (7%)
  starting transfers between devices  24.4 us (5%)
  between operations  14.6 us (3%)
    reduce_scatter x2, waiting for transfers between devices, sum_columns(): lax.psum_scatter(term.astype(jnp.bfloat16), 'head', scatter_dimension=2,...  110 us
    all_to_all x1, blocking collectives, to_time(): lax.all_to_all(stacked, 'head', split_axis=1, concat_axis=2, tiled=True)  73.8 us
    all_to_all x2, waiting for transfers between devices, to_heads(): lax.all_to_all(jnp.stack(jnp.split(stacked, lax.axis_size('head'), axis=2...  42.8 us
    unnamed x5, waiting for transfers between devices  40.7 us
    dot_general x8, matrix products, one_block(): jnp.einsum('qhe,khe->hqk', query_part, key_part, precision=lax.Precision....  23.7 us
    reduce_scatter x1, waiting for transfers between devices, sum_rows(): lax.psum_scatter(term.astype(jnp.bfloat16), 'seq', scatter_dimension=1, t...  21.9 us
    dot_general x6, matrix products, one_block(): jnp.einsum('hqk,khe->qhe', weights, value_part, precision=lax.Precision.H...  21.4 us
    unnamed x47, local copies, waits for them, and re-layouts  17.4 us
  transfers between devices with their start and end apart: 11, of which 5 were waited for; matrix products, arithmetic and copies ran while one was open for 22% of the time, Pallas kernels for 0%

profile of v1, /device:TPU:0, one launch (start us, length us, event | category | flops | bytes accessed | tf_op | source)
XLA Modules:
  0.0 511.4 jit_solution(12847431635841830650)
XLA Ops:
  8.8 1.8 fusion.39
  11.5 6.3 %all-to-all-start.2 = ((bf16[4,1,256,256]{3,2,1,0:T(8,128)(2,1)}), bf16[4,1,256,256]{3,2,1,0:T(8,128)(2,1)S(1)}, u32[]{:S(2)}, u32[]{:S(2)}) async-start(bf16[4,1,256,256]{3,2,1,0:T(8,128)(2,1)} %pad_maximum_fusion.4), calls=%async_computation.2 | async-start | bytes 1048576 | tf_op jit(solution)/shard_map/all_to_all | solution.py:88
  18.8 4.7 fusion.34
  25.0 7.3 %all-to-all-done.2 = bf16[4,1,256,256]{3,2,1,0:T(8,128)(2,1)S(1)} async-done(((bf16[4,1,256,256]{3,2,1,0:T(8,128)(2,1)}), bf16[4,1,256,256]{3,2,1,0:T(8,128)(2,1)S(1)}, u32[]{:S(2)}, u32[]{:S(2)}) %all-to-all-start.2) | async-done | bytes 524320 | tf_op jit(solution)/shard_map/all_to_all | solution.py:88
  32.3 4.3 all-to-all-start
  37.7 35.5 %all-to-all-done = bf16[4,3,256,256]{3,2,1,0:T(8,128)(2,1)} async-done(((bf16[4,3,256,256]{3,2,1,0:T(8,128)(2,1)}), bf16[4,3,256,256]{3,2,1,0:T(8,128)(2,1)}, u32[]{:S(2)}, u32[]{:S(2)}) %all-to-all-start) | async-done | bytes 1572896 | tf_op jit(solution)/shard_map/all_to_all | solution.py:88
  80.1 2.5 copy.66
  84.0 2.8 copy.65
  88.2 30.1 %while.32 = (s32[]{:T(128)}, bf16[2,512,256]{2,1,0:T(8,128)(2,1)}, s32[2]{0:T(128)S(1)}, f32[1280,256]{0,1:T(8,128)}, s32[]{:T(128)}, /*index=5*/f32[1024,256]{0...) while((s32[]{:T(128)}, bf16[2,512,256]{2,1,0:T(8,128)(2,1)}, ...), condition=%wide.region_5.6_spmd, body=%wide.region_2.5_spmd.sunk | while | flops 2426537472 | bytes 25986388 | solution.py:75
  90.6 2.4 constant_dynamic-slice_fusion.15
  94.0 3.3 fusion.114
  98.5 4.0 fusion.116
  105.4 2.4 constant_dynamic-slice_fusion.15
  108.8 3.3 fusion.114
  113.3 4.0 fusion.116
  118.3 1.9 copy.108
  120.7 4.6 reduce.4
  125.3 2.0 reshape.389
  127.3 4.1 all-to-all-start.1
  134.9 59.8 %while.33 = (s32[]{:T(128)}, f32[1024,256]{1,0:T(8,128)}, f32[1280,256]{0,1:T(8,128)}, f32[1280,256]{0,1:T(8,128)}, s32[2]{0:T(128)S(1)}, /*index=5*/f32[2,512,2...) while((s32[]{:T(128)}, f32[1024,256]{1,0:T(8,128)}, ...), condition=%wide.region_10.11_spmd, body=%wide.region_6.10_spmd.sunk | while | flops 6061953024 | bytes 89728512 | solution.py:75
  141.3 3.3 fusion.130
  146.0 3.9 multiply_reduce_fusion.2
  151.2 1.9 fusion.134
  153.2 2.8 fusion.133
  156.3 3.4 fusion.132
  171.0 3.3 fusion.130
  175.7 3.9 multiply_reduce_fusion.2
  180.9 1.9 fusion.134
  182.9 2.8 fusion.133
  186.0 3.4 fusion.132
  194.7 3.9 copy.89
  198.6 2.2 copy.90
  200.8 2.2 reshape.390
  205.1 3.3 fusion.29
  208.5 4.0 fusion.27
  212.7 5.6 %collective-permute-start.2 = (bf16[2,128,256]{2,0,1:T(2,128)(2,1)S(1)}, bf16[2,128,256]{2,0,1:T(2,128)(2,1)S(1)}, u32[]{:S(2)}, u32[]{:S(2)}) collective-permute-start(bf16[2,128,256]{2,0,1:T(2,128)(2,1)S(1)} %get-tuple-element.462), channel_id=1, source_target_pairs={{0,4},{4,8},{8,12},{12,16},{16,20},{20,24},{24,28},{1,5},{5,9},{9,... | collective-permute-start | bytes 393224 | tf_op jit(solution)/shard_map/ppermute | solution.py:19
  220.5 1.9 fusion.28
  224.0 2.2 pad_maximum_fusion.1
  226.2 73.8 %all_to_all.43 = bf16[3,1024,256]{2,0,1:T(4,128)(2,1)S(1)} all-to-all(bf16[3,1024,256]{2,0,1:T(4,128)(2,1)S(1)} %pad_maximum_fusion.1), channel_id=1, replica_groups=mesh['seq'=8,'head'=4] {'head'}, dimensions={1} | all-to-all | bytes 3145728 | tf_op jit(solution)/shard_map/all_to_all | solution.py:94
  300.1 2.6 copy.107
  302.7 3.8 all_to_all.38
  306.5 6.1 %fusion.26 = bf16[3,1024,1024]{1,2,0:T(8,128)(2,1)} fusion(bf16[3,256,1024]{2,1,0:T(8,128)(2,1)} %all_to_all.38, bf16[256,1024]{1,0:T(8,128)(2,1)S(1)} %copy-done.14, f32[1024]{0:T(1024)S(1)} %copy-done.28, f32[256]{0:T(256)S(1)} %copy-done.24, f32[256]{0:T(256)S(1)} %copy-done.22), kind=kOutput, calls=%fused_computation.55 | convolution fusion | flops 1618214912 | bytes 8394752 | tf_op jit(solution)/shard_map/td,ctf->cdf/dot_general | solution.py:159
  313.4 109.6 %reduce-scatter.7.cloned.1.call-done = bf16[3,1024,256]{1,2,0:T(8,128)(2,1)} async-done(((bf16[3,1024,1024]{1,2,0:T(8,128)(2,1)}), bf16[3,1024,256]{1,2,0:T(8,128)(2,1)}) %reduce-scatter.7.cloned.1.call-update) | async-done | bytes 1572880 | tf_op jit(solution)/shard_map/reduce_scatter | solution.py:98
  423.0 4.4 copy.91
  427.4 3.2 copy.104
  432.1 5.1 fusion.43
  438.8 21.9 %reduce-scatter.11.cloned.1.call-done = bf16[1,128,256]{2,1,0:T(8,128)(2,1)} async-done(((bf16[1,1024,256]{2,1,0:T(8,128)(2,1)}), bf16[1,128,256]{2,1,0:T(8,128)(2,1)}) %reduce-scatter.11.cloned.1.call-update) | async-done | bytes 65552 | tf_op jit(solution)/shard_map/reduce_scatter | solution.py:104
  462.3 40.0 %reduce-scatter.13.cloned.1.call-done = bf16[128,768]{1,0:T(8,128)(2,1)} async-done(((bf16[1024,768]{1,0:T(8,128)(2,1)}), bf16[128,768]{1,0:T(8,128)(2,1)}) %reduce-scatter.13.cloned.1.call-update) | async-done | bytes 196624
  (196 shorter events, 69.2 us)
Async XLA Ops:
  7.2 1.6 copy-start
  7.2 10.6 %copy-start.13 = (bf16[256,1024]{1,0:T(8,128)(2,1)S(1)}, bf16[256,1024]{1,0:T(8,128)(2,1)}, u32[]{:S(2)}) copy-start(bf16[256,1024]{1,0:T(8,128)(2,1)} %param.13) | copy-start | bytes 1572868
  10.5 8.2 %copy-start.27 = (f32[1024]{0:T(1024)S(1)}, f32[1024]{0:T(1024)}, u32[]{:S(2)}) copy-start(f32[1024]{0:T(1024)} %param.15) | copy-start | bytes 12292
  11.5 20.8 %all-to-all-start.2 = ((bf16[4,1,256,256]{3,2,1,0:T(8,128)(2,1)}), bf16[4,1,256,256]{3,2,1,0:T(8,128)(2,1)S(1)}, u32[]{:S(2)}, u32[]{:S(2)}) async-start(bf16[4,1,256,256]{3,2,1,0:T(8,128)(2,1)} %pad_maximum_fusion.4), calls=%async_computation.2 | async-start | bytes 1048576 | tf_op jit(solution)/shard_map/all_to_all | solution.py:88
  18.0 5.5 %copy-start.21 = (f32[256]{0:T(256)}, f32[256]{0:T(256)S(1)}, u32[]{:S(2)}) copy-start(f32[256]{0:T(256)S(1)} %broadcast_multiply_fusion) | copy-start | bytes 3076
  18.8 4.7 copy-start.23
  32.3 40.9 %all-to-all-start = ((bf16[4,3,256,256]{3,2,1,0:T(8,128)(2,1)}), bf16[4,3,256,256]{3,2,1,0:T(8,128)(2,1)}, u32[]{:S(2)}, u32[]{:S(2)}) async-start(bf16[4,3,256,256]{3,2,1,0:T(8,128)(2,1)} %pad_maximum_fusion.2), calls=%async_computation | async-start | bytes 3145728 | tf_op jit(solution)/shard_map/all_to_all | solution.py:88
  76.4 6.2 %collective-permute-start = (bf16[2,128,256]{2,1,0:T(8,128)(2,1)}, bf16[2,128,256]{2,1,0:T(8,128)(2,1)S(1)}, u32[]{:S(2)}, u32[]{:S(2)}) collective-permute-start(bf16[2,128,256]{2,1,0:T(8,128)(2,1)} %get-tuple-element.466), channel_id=1, source_target_pairs={{0,4},{4,8},{8,12},{12,16},{16,20},{20,24},{24,28},{1,5},{5,9},{9,... | collective-permute-start | bytes 393224 | tf_op jit(solution)/shard_map/ppermute | solution.py:19
  77.7 5.0 collective-permute-start.1
  97.4 1.1 copy-start.12
  98.5 4.2 copy-start.19
  102.7 0.8 copy-start.20
  112.1 1.1 copy-start.12
  113.3 4.2 copy-start.19
  127.3 73.5 %all-to-all-start.1 = ((bf16[4,2,32768]{2,1,0:T(2,128)(2,1)}), bf16[4,2,32768]{2,1,0:T(2,128)(2,1)}, u32[]{:S(2)}, u32[]{:S(2)}) async-start(bf16[4,2,32768]{2,1,0:T(2,128)(2,1)} %reshape.389), calls=%async_computation.1 | async-start | bytes 1048576 | tf_op jit(solution)/shard_map/all_to_all | solution.py:94
  131.4 181.3 %reduce-scatter.9.cloned.1.call-start = ((), (), s32[]{:S(2)}) async-start(), calls=%async_computation.9 | async-start | bytes 2621440 | tf_op jit(solution)/shard_map/reduce_scatter | solution.py:98
  144.6 1.3 copy-start.1
  144.6 1.4 copy-start.2
  153.1 2.8 copy-start.3
  153.1 2.8 copy-start.5
  156.3 3.4 copy-start.4
  156.3 3.4 copy-start.6
  156.3 3.4 copy-start.8
  174.3 1.3 copy-start.1
  174.3 1.4 copy-start.2
  182.8 2.8 copy-start.3
  182.9 2.8 copy-start.5
  186.0 3.4 copy-start.4
  186.0 3.4 copy-start.6
  186.0 3.4 copy-start.8
  194.7 3.9 copy-start.7
  205.1 3.3 copy-start.15
  208.5 11.1 %copy-start.9 = (f32[1024,256]{1,0:T(8,128)S(1)}, f32[1024,256]{1,0:T(8,128)}, u32[]{:S(2)}) copy-start(f32[1024,256]{1,0:T(8,128)} %get-tuple-element.325) | copy-start | bytes 3145732
  208.5 214.5 %reduce-scatter.7.cloned.1.call-start = ((), (), s32[]{:S(2)}) async-start(), calls=%async_computation.8 | async-start | bytes 7864320 | tf_op jit(solution)/shard_map/reduce_scatter | solution.py:98
  212.5 8.0 %copy-start.10 = (f32[1,1280,256]{2,0,1:T(1,128)S(1)}, f32[1,1280,256]{2,0,1:T(1,128)}, u32[]{:S(2)}) copy-start(f32[1,1280,256]{2,0,1:T(1,128)} %copy.89) | copy-start | bytes 3932164
  212.5 8.0 %copy-start.11 = (f32[1,1280,256]{2,0,1:T(1,128)S(1)}, f32[1,1280,256]{2,0,1:T(1,128)}, u32[]{:S(2)}) copy-start(f32[1,1280,256]{2,0,1:T(1,128)} %copy.90) | copy-start | bytes 3932164
  212.7 9.8 %collective-permute-start.2 = (bf16[2,128,256]{2,0,1:T(2,128)(2,1)S(1)}, bf16[2,128,256]{2,0,1:T(2,128)(2,1)S(1)}, u32[]{:S(2)}, u32[]{:S(2)}) collective-permute-start(bf16[2,128,256]{2,0,1:T(2,128)(2,1)S(1)} %get-tuple-element.462), channel_id=1, source_target_pairs={{0,4},{4,8},{8,12},{12,16},{16,20},{20,24},{24,28},{1,5},{5,9},{9,... | collective-permute-start | bytes 393224 | tf_op jit(solution)/shard_map/ppermute | solution.py:19
  218.3 4.2 collective-permute-start.3
  300.1 6.5 %copy-start.14 = (bf16[256,1024]{1,0:T(8,128)(2,1)S(1)}, bf16[256,1024]{1,0:T(8,128)(2,1)}, u32[]{:S(2)}) copy-start(bf16[256,1024]{1,0:T(8,128)(2,1)} %param.13) | copy-start | bytes 1572868
  300.1 6.5 %copy-start.22 = (f32[256]{0:T(256)S(1)}, f32[256]{0:T(256)}, u32[]{:S(2)}) copy-start(f32[256]{0:T(256)} %copy-done.21) | copy-start | bytes 3076
  300.1 6.5 %copy-start.24 = (f32[256]{0:T(256)S(1)}, f32[256]{0:T(256)}, u32[]{:S(2)}) copy-start(f32[256]{0:T(256)} %copy-done.23) | copy-start | bytes 3076
  300.1 6.5 %copy-start.28 = (f32[1024]{0:T(1024)S(1)}, f32[1024]{0:T(1024)}, u32[]{:S(2)}) copy-start(f32[1024]{0:T(1024)} %param.15) | copy-start | bytes 12292
  312.6 148.2 %reduce-scatter.11.cloned.1.call-start = ((), (), s32[]{:S(2)}) async-start(), calls=%async_computation.10 | async-start | bytes 589824 | tf_op jit(solution)/shard_map/reduce_scatter | solution.py:104
  313.4 188.9 %reduce-scatter.13.cloned.1.call-start = ((), (), s32[]{:S(2)}) async-start(), calls=%async_computation.11 | async-start | bytes 1769472
  427.4 3.2 copy-start.16
  430.6 1.5 copy-start.18
  432.1 5.1 copy-start.26
  432.1 5.5 %copy-start.17 = (bf16[256,1024]{1,0:T(8,128)(2,1)S(1)}, bf16[256,1024]{1,0:T(8,128)(2,1)}, u32[]{:S(2)}) copy-start(bf16[256,1024]{1,0:T(8,128)(2,1)} %param.14) | copy-start | bytes 1572868
  (2 other events, 1.3 us)
Sparse Core Ops, SparseCore 0:
  208.6 66.3 reduce-scatter.8
  312.8 110.2 reduce-scatter.6
  426.1 34.6 reduce-scatter.10
  463.9 38.3 reduce-scatter.12
